TPU v7x, 256 devices: a whole 4x4x8 slice. The times are simulated.
256 devices in a mesh: dp: 32 (over z, x), pipe: 2 (over core), tensor: 4 (over y).
Axes of the slice: x: 4, y: 4, z: 8, core: 2. Of those that a mesh axis runs over, the one named last changes fastest.
Arguments:
- tokens: bfloat16 [64, 64, 4096], P('dp', None, 'tensor'), may hold values from -8 to 8
- w_query: bfloat16 [2, 2, 4096, 4096], P(None, 'pipe', 'dp', 'tensor'), may hold values from -8 to 8
- w_key: bfloat16 [2, 2, 4096, 1024], P(None, 'pipe', 'dp', 'tensor'), may hold values from -1 to 1
- w_value: bfloat16 [2, 2, 4096, 1024], P(None, 'pipe', 'dp', 'tensor'), may hold values from -0.09375 to 0.09375
- w_out: bfloat16 [2, 2, 4096, 4096], P(None, 'pipe', 'tensor', 'dp'), may hold values from -0.09375 to 0.09375
- norm_gain: float32 [2, 2, 4096], P(None, 'pipe'), may hold values from 0.5 to 1.5
- boundary: int32 [64], P('dp'), may hold values from 1 to 63
- skip_offset: int32 [64], P('dp'), may hold values from 0 to 131008
- doc_lengths: int32 [64, 4], P('dp'), may hold values from 1 to 32, 64 in all within a row
- batch_order: int32 [32, 2], P('dp'), may hold values from 0 to 1, each once within a row
Outputs:
- final_state: bfloat16 [64, 64, 4096], P('dp', 'pipe', 'tensor')
Inputs may be any that keep to these rules, and one draw needn't show every extreme that they name: `doc_lengths`: each row sums to 64. `batch_order`: each row is a permutation.
All inputs are finite; a program needn't handle non-finite values.
Results may differ from a plain program's by a relative error of at most 0.014.
Values may be sent and summed in bfloat16 or wider, within the bound.
A program may use at most 192 MiB of HBM per device.

v0:
```python
from functools import partial
import jax
import jax.numpy as jnp
from jax import lax
from jax.sharding import PartitionSpec as P

HEAD_DIM = 128
ROPE_THETA = 500000.0
NORM_EPSILON = 1e-05


def cut_along(value, dim, peers):
    before, after = (value.shape[:dim], value.shape[dim + 1 :])
    return jnp.moveaxis(value.reshape(*before, peers, -1, *after), dim, 0)


def sent_and_summed(value, axis, dim):
    peers = lax.axis_size(axis)
    blocks = lax.all_to_all(cut_along(value, dim, peers), axis, 0, 0, tiled=True)
    return jnp.sum(blocks, axis=0)


def sent_together(arrays, axis, dim, along):
    widths = [a.shape[along] for a in arrays]
    both = jnp.concatenate(arrays, axis=along)
    whole = lax.all_gather(both, axis, axis=dim, tiled=True)
    return tuple(jnp.split(whole, [sum(widths[:k]) for k in range(1, len(widths))], axis=along))


def from_behind(value, axis, by):
    peers = lax.axis_size(axis)
    pairs = [(i, i + by) for i in range(peers) if 0 <= i + by < peers]
    return lax.ppermute(value, axis, pairs)


def picked(value, axis, root):
    return lax.dynamic_index_in_dim(lax.all_gather(value, axis), root, 0, keepdims=False)


def rope_angles(positions, head_dim):
    half_dim = head_dim // 2
    exponent = jnp.arange(half_dim, dtype=jnp.float32) * (2.0 / head_dim)
    frequency = jnp.float32(ROPE_THETA) ** (-exponent)
    return positions.astype(jnp.float32)[..., None] * frequency


def rotate(values, angles):
    half_dim = values.shape[-1] // 2
    first_half = values[..., :half_dim]
    second = values[..., half_dim:]
    cosine = jnp.cos(angles)[:, None, :]
    sine_part = jnp.sin(angles)[:, None, :]
    return jnp.concatenate(
        [first_half * cosine - second * sine_part, second * cosine + first_half * sine_part],
        axis=-1,
    )


def sample_layout(first_cut, offset, lengths, seq_len):
    places = jnp.arange(seq_len, dtype=jnp.int32)
    positions = jnp.where(places < first_cut, places, places + offset)
    doc_ends = jnp.cumsum(lengths)
    doc_ids = jnp.sum((places[:, None] >= doc_ends[None, :]).astype(jnp.int32), axis=1)
    allowed = (doc_ids[:, None] == doc_ids[None, :]) & (places[None, :] <= places[:, None])
    return (positions, allowed)


def attend(normed, q_weight, k_weight, v_weight, angles, allowed):
    seq_len = normed.shape[0]
    q_heads = q_weight.shape[1] // HEAD_DIM
    kv_heads = k_weight.shape[1] // HEAD_DIM
    group_size = q_heads // kv_heads
    queries = jnp.dot(normed, q_weight, preferred_element_type=jnp.float32)
    key_vecs = jnp.dot(normed, k_weight, preferred_element_type=jnp.float32)
    value_vecs = jnp.dot(normed, v_weight, preferred_element_type=jnp.float32).astype(jnp.bfloat16)
    value_vecs = value_vecs.reshape(seq_len, kv_heads, HEAD_DIM)
    queries = rotate(queries.reshape(seq_len, q_heads, HEAD_DIM), angles).astype(jnp.bfloat16)
    queries = queries.reshape(seq_len, kv_heads, group_size, HEAD_DIM)
    key_vecs = rotate(key_vecs.reshape(seq_len, kv_heads, HEAD_DIM), angles).astype(jnp.bfloat16)
    scores = jnp.einsum(
        "skgd,tkd->kgst", queries, key_vecs, preferred_element_type=jnp.float32
    ) * HEAD_DIM ** (-0.5)
    scores = jnp.where(allowed[None, None], scores, -jnp.inf)
    row_max = jnp.max(scores, axis=-1, keepdims=True)
    exp_scores = jnp.exp(scores - row_max)
    weights = (exp_scores / jnp.sum(exp_scores, axis=-1, keepdims=True)).astype(jnp.bfloat16)
    mixed = jnp.einsum("kgst,tkd->skgd", weights, value_vecs, preferred_element_type=jnp.float32)
    return mixed.reshape(seq_len, q_heads * HEAD_DIM)


def layer_step(stream, active, gain_row, weight_three, out_part, angles, allowed):
    gathered = lax.all_gather(stream, "tensor", axis=1, tiled=True)
    seq_len = gathered.shape[0]
    head_width = weight_three[0].shape[1]

    def local_mix():
        widened = gathered.astype(jnp.float32)
        inv_rms = lax.rsqrt(jnp.mean(widened * widened, axis=-1, keepdims=True) + NORM_EPSILON)
        normed = (widened * inv_rms * gain_row).astype(jnp.bfloat16)
        return attend(
            normed, weight_three[0], weight_three[1], weight_three[2], angles, allowed
        ).astype(jnp.bfloat16)

    mixed = lax.cond(active, local_mix, lambda: jnp.zeros((seq_len, head_width), jnp.bfloat16))
    partial_sum = lax.cond(
        active,
        lambda: jnp.dot(mixed, out_part, preferred_element_type=jnp.float32),
        lambda: jnp.zeros((mixed.shape[0], out_part.shape[1]), jnp.float32),
    )
    shares = sent_and_summed(partial_sum, "tensor", 1)
    updated = (stream.astype(jnp.float32) + shares).astype(jnp.bfloat16)
    return jnp.where(active, updated, jnp.zeros_like(updated))


def per_device(
    tokens,
    w_query,
    w_key,
    w_value,
    w_out,
    norm_gain,
    boundary,
    skip_offset,
    doc_lengths,
    batch_order,
):
    sections = lax.axis_size("pipe")
    my_section = lax.axis_index("pipe")
    micro_count = tokens.shape[0]
    seq_len = tokens.shape[1]
    local_width = tokens.shape[2]
    ordered = batch_order[0]
    doc_costs = jnp.sum(doc_lengths * doc_lengths, axis=1)
    slot_cost = jnp.take(doc_costs, ordered)
    slot_of = jnp.argsort(-slot_cost, stable=True)
    samples = jnp.take(ordered, slot_of)
    feed_rows = jnp.take(tokens, samples, axis=0)
    positions, allowed = jax.vmap(partial(sample_layout, seq_len=seq_len))(
        jnp.take(boundary, samples),
        jnp.take(skip_offset, samples),
        jnp.take(doc_lengths, samples, axis=0),
    )
    angles = rope_angles(positions, HEAD_DIM)
    down_gain = norm_gain[0, 0]
    up_gain = norm_gain[1, 0]
    out_full = lax.all_gather(w_out, "dp", axis=3, tiled=True)
    down_out_part = out_full[0, 0]
    up_out_part = out_full[1, 0]
    query_full, key_full, value_full = sent_together((w_query, w_key, w_value), "dp", 2, 3)
    down_three = (query_full[0, 0], key_full[0, 0], value_full[0, 0])
    up_three = (query_full[1, 0], key_full[1, 0], value_full[1, 0])
    step_count = micro_count + 2 * sections - 2
    empty_rows = jnp.zeros((seq_len, local_width), jnp.bfloat16)
    last_item = micro_count - 1

    def select_item(stacked, item_index):
        return lax.dynamic_index_in_dim(
            stacked, jnp.clip(item_index, 0, last_item), 0, keepdims=False
        )

    def advance(tick_now, loop_state):
        down_buf, up_buf, results, up_weights = loop_state
        down_item = tick_now - my_section
        down_ok = (down_item >= 0) & (down_item < micro_count)
        down_in = jnp.where(my_section == 0, select_item(feed_rows, tick_now), down_buf)
        down_out = layer_step(
            down_in,
            down_ok,
            down_gain,
            down_three,
            down_out_part,
            select_item(angles, down_item),
            select_item(allowed, down_item),
        )
        up_item = tick_now - (2 * sections - 2 - my_section)
        up_ok = (up_item >= 0) & (up_item < micro_count)
        up_in = jnp.where(my_section == sections - 1, down_out, up_buf)
        up_out = layer_step(
            up_in,
            up_ok,
            up_gain,
            up_weights,
            up_out_part,
            select_item(angles, up_item),
            select_item(allowed, up_item),
        )
        out_slot = select_item(slot_of, up_item)
        stored = lax.dynamic_update_index_in_dim(results, up_out, out_slot, 0)
        results = jnp.where(up_ok & (my_section == 0), stored, results)
        down_buf = from_behind(down_out, "pipe", 1)
        up_buf = from_behind(up_out, "pipe", -1)
        return (down_buf, up_buf, results, up_weights)

    initial = (
        empty_rows,
        empty_rows,
        jnp.zeros((micro_count, seq_len, local_width), jnp.bfloat16),
        up_three,
    )
    down_buf, up_buf, results, up_weights = lax.fori_loop(0, step_count, advance, initial)
    spread = picked(results, "pipe", 0)
    row_count = seq_len // sections
    return lax.dynamic_slice_in_dim(spread, my_section * row_count, row_count, 1)


def solution(mesh):
    placed = (
        P("dp", None, "tensor"),
        P(None, "pipe", "dp", "tensor"),
        P(None, "pipe", "dp", "tensor"),
        P(None, "pipe", "dp", "tensor"),
        P(None, "pipe", "tensor", "dp"),
        P(None, "pipe", None),
        P("dp"),
        P("dp"),
        P("dp", None),
        P("dp", None),
    )
    return jax.shard_map(
        per_device, mesh=mesh, in_specs=placed, out_specs=P("dp", "pipe", "tensor"), check_vma=False
    )
```

profile of v0, /device:TPU:1, one launch (start us, length us, event | category | flops | bytes accessed | tf_op | source)
XLA Modules:
  0.0 725.0 jit_solution(7644802526432635606)
XLA Ops:
  22.8 136.4 %all-gather.6.cloned.1.call-done = bf16[2,1,1024,4096]{3,2,1,0:T(8,128)(2,1)} async-done(((bf16[2,1,1024,128]{3,2,1,0:T(8,128)(2,1)}), bf16[2,1,1024,4096]{3,2,1,0:T(8,128)(2,1)}) %all-gather.6.cloned.1.call-update) | async-done | bytes 16777232 | tf_op jit(solution)/shard_map/all_gather | solution.py:146
  159.2 11.7 %slice_bitcast_fusion = (bf16[1024,4096]{1,0:T(8,128)(2,1)}, bf16[1024,4096]{1,0:T(8,128)(2,1)}) fusion(bf16[2,1,1024,4096]{3,2,1,0:T(8,128)(2,1)} %all-gather.6.cloned.1.call-done), kind=kLoop, calls=%fused_computation.98 | loop fusion | bytes 33554432 | tf_op jit(solution)/shard_map/squeeze | solution.py:148
  170.9 174.1 %all-gather.4.cloned.1.call-done = bf16[2,1,4096,1536]{3,2,1,0:T(8,128)(2,1)} async-done(((bf16[2,1,128,1536]{3,2,1,0:T(8,128)(2,1)}), bf16[2,1,4096,1536]{3,2,1,0:T(8,128)(2,1)}) %all-gather.4.cloned.1.call-update) | async-done | bytes 25165840 | tf_op jit(solution)/shard_map/all_gather | solution.py:26
  351.3 11.6 %slice_bitcast_fusion.1 = (bf16[4096,1024]{1,0:T(8,128)(2,1)}, bf16[4096,1024]{1,0:T(8,128)(2,1)}) fusion(bf16[2,1,4096,1536]{3,2,1,0:T(8,128)(2,1)} %all-gather.4.cloned.1.call-done), kind=kLoop, calls=%fused_computation.99 | loop fusion | bytes 33554432 | tf_op jit(solution)/shard_map/squeeze | solution.py:151
  363.6 351.6 %while.19 = (s32[]{:T(128)}, bf16[64,1024]{1,0:T(8,128)(2,1)}, bf16[64,1024]{1,0:T(8,128)(2,1)S(1)}, bf16[2,64,1024]{2,1,0:T(8,128)(2,1)S(1)}, s32[]{:T(128)}, /...) while((s32[]{:T(128)}, bf16[64,1024]{1,0:T(8,128)(2,1)}, ...), condition=%wide.region_21.23_spmd.clone, body=%wide.region_4.22_spmd.clone.sunk | while | flops 2746410496 | bytes 85502200 | solution.py:200
  364.6 11.5 %all_gather.36 = bf16[64,4096]{1,0:T(8,128)(2,1)S(1)} all-gather(bf16[64,1024]{1,0:T(8,128)(2,1)S(1)} %bitcast_select_fusion.3), channel_id=1, replica_groups=mesh['dp'=32,'pipe'=2,'tensor'=4] {'tensor'}, dimensions={1}, use_global_device_ids=true | all-gather | bytes 655360 | tf_op jit(solution)/shard_map/while/body/eval_jaxpr/all_gather | solution.py:92
  383.7 9.7 %all-to-all-done = f32[4,64,1024]{2,1,0:T(8,128)S(1)} async-done(((f32[4,64,1024]{2,1,0:T(8,128)}), f32[4,64,1024]{2,1,0:T(8,128)S(1)}, u32[]{:S(2)}, u32[]{:S(2)}) %all-to-all-start) | async-done | bytes 1048608 | tf_op jit(solution)/shard_map/while/body/eval_jaxpr/all_to_all | solution.py:19
  394.2 9.9 %all_gather.37 = bf16[64,4096]{1,0:T(8,128)(2,1)S(1)} all-gather(bf16[64,1024]{1,0:T(8,128)(2,1)S(1)} %get-tuple-element.869), channel_id=1, replica_groups=mesh['dp'=32,'pipe'=2,'tensor'=4] {'tensor'}, dimensions={1}, use_global_device_ids=true | all-gather | bytes 655360 | tf_op jit(solution)/shard_map/while/body/eval_jaxpr/all_gather | solution.py:92
  413.6 6.4 all-to-all-done.1
  420.2 26.8 %collective-permute-start.1 = (bf16[64,1024]{1,0:T(8,128)(2,1)S(1)}, bf16[64,1024]{1,0:T(8,128)(2,1)S(1)}, u32[]{:S(2)}, u32[]{:S(2)}) collective-permute-start(bf16[64,1024]{1,0:T(8,128)(2,1)S(1)} %get-tuple-element.870), channel_id=1, source_target_pairs={{4,0},{5,1},{6,2},{7,3},{12,8},{13,9},{14,10},{15,11},{20,16},{21,... | collective-permute-start | bytes 393224 | tf_op jit(solution)/shard_map/while/body/eval_jaxpr/ppermute | solution.py:33
  448.9 9.9 %all_gather.36 = bf16[64,4096]{1,0:T(8,128)(2,1)S(1)} all-gather(bf16[64,1024]{1,0:T(8,128)(2,1)S(1)} %bitcast_select_fusion.3), channel_id=1, replica_groups=mesh['dp'=32,'pipe'=2,'tensor'=4] {'tensor'}, dimensions={1}, use_global_device_ids=true | all-gather | bytes 655360 | tf_op jit(solution)/shard_map/while/body/eval_jaxpr/all_gather | solution.py:92
  460.4 11.3 %conditional.12 = (bf16[64,1024]{1,0:T(8,128)(2,1)S(1)}) conditional(s32[]{:T(128)} %convert_element_type.206, () %tuple.107, (bf16[64,4096]{1,0:T(8,128)(2,1)S(1)}, f32[1,1,4096]{2,1,0:T(1,128)S(1)}, bf16[4096,256]{1,0:T(8,128)(2,1)}, s32[]{:T(128)}, pred[2,64,64]{1,2,0:T(8,128)(4,1)S(1)}, /*index=5*/bf16[4096,256]{1,0:T(8,128)(2,1)}, ...), branch_computations={%region_5.6_spmd, %region_6.10_spmd} | conditional | flops 835764928 | bytes 17847848 | solution.py:104
  482.6 11.3 %all-to-all-done = f32[4,64,1024]{2,1,0:T(8,128)S(1)} async-done(((f32[4,64,1024]{2,1,0:T(8,128)}), f32[4,64,1024]{2,1,0:T(8,128)S(1)}, u32[]{:S(2)}, u32[]{:S(2)}) %all-to-all-start) | async-done | bytes 1048608 | tf_op jit(solution)/shard_map/while/body/eval_jaxpr/all_to_all | solution.py:19
  494.7 10.7 %all_gather.37 = bf16[64,4096]{1,0:T(8,128)(2,1)S(1)} all-gather(bf16[64,1024]{1,0:T(8,128)(2,1)S(1)} %get-tuple-element.869), channel_id=1, replica_groups=mesh['dp'=32,'pipe'=2,'tensor'=4] {'tensor'}, dimensions={1}, use_global_device_ids=true | all-gather | bytes 655360 | tf_op jit(solution)/shard_map/while/body/eval_jaxpr/all_gather | solution.py:92
  505.4 11.5 %conditional.14 = (bf16[64,1024]{1,0:T(8,128)(2,1)S(1)}) conditional(s32[]{:T(128)} %convert_element_type.207, () %tuple.111, (bf16[64,4096]{1,0:T(8,128)(2,1)S(1)}, f32[1,1,4096]{2,1,0:T(1,128)S(1)}, bf16[4096,256]{1,0:T(8,128)(2,1)}, pred[2,64,64]{1,2,0:T(8,128)(4,1)S(1)}, s32[]{:T(128)}, /*index=5*/bf16[4096,256]{1,0:T(8,128)(2,1)}, ...), branch_computations={%region_13.14_spmd, %region_14.18_spmd} | conditional | flops 835764928 | bytes 26319488 | solution.py:104
  540.9 9.9 %all_gather.36 = bf16[64,4096]{1,0:T(8,128)(2,1)S(1)} all-gather(bf16[64,1024]{1,0:T(8,128)(2,1)S(1)} %bitcast_select_fusion.3), channel_id=1, replica_groups=mesh['dp'=32,'pipe'=2,'tensor'=4] {'tensor'}, dimensions={1}, use_global_device_ids=true | all-gather | bytes 655360 | tf_op jit(solution)/shard_map/while/body/eval_jaxpr/all_gather | solution.py:92
  552.4 11.3 %conditional.12 = (bf16[64,1024]{1,0:T(8,128)(2,1)S(1)}) conditional(s32[]{:T(128)} %convert_element_type.206, () %tuple.107, (bf16[64,4096]{1,0:T(8,128)(2,1)S(1)}, f32[1,1,4096]{2,1,0:T(1,128)S(1)}, bf16[4096,256]{1,0:T(8,128)(2,1)}, s32[]{:T(128)}, pred[2,64,64]{1,2,0:T(8,128)(4,1)S(1)}, /*index=5*/bf16[4096,256]{1,0:T(8,128)(2,1)}, ...), branch_computations={%region_5.6_spmd, %region_6.10_spmd} | conditional | flops 835764928 | bytes 17847848 | solution.py:104
  574.5 10.6 %all-to-all-done = f32[4,64,1024]{2,1,0:T(8,128)S(1)} async-done(((f32[4,64,1024]{2,1,0:T(8,128)}), f32[4,64,1024]{2,1,0:T(8,128)S(1)}, u32[]{:S(2)}, u32[]{:S(2)}) %all-to-all-start) | async-done | bytes 1048608 | tf_op jit(solution)/shard_map/while/body/eval_jaxpr/all_to_all | solution.py:19
  586.0 9.9 %all_gather.37 = bf16[64,4096]{1,0:T(8,128)(2,1)S(1)} all-gather(bf16[64,1024]{1,0:T(8,128)(2,1)S(1)} %get-tuple-element.869), channel_id=1, replica_groups=mesh['dp'=32,'pipe'=2,'tensor'=4] {'tensor'}, dimensions={1}, use_global_device_ids=true | all-gather | bytes 655360 | tf_op jit(solution)/shard_map/while/body/eval_jaxpr/all_gather | solution.py:92
  595.8 11.5 %conditional.14 = (bf16[64,1024]{1,0:T(8,128)(2,1)S(1)}) conditional(s32[]{:T(128)} %convert_element_type.207, () %tuple.111, (bf16[64,4096]{1,0:T(8,128)(2,1)S(1)}, f32[1,1,4096]{2,1,0:T(1,128)S(1)}, bf16[4096,256]{1,0:T(8,128)(2,1)}, pred[2,64,64]{1,2,0:T(8,128)(4,1)S(1)}, s32[]{:T(128)}, /*index=5*/bf16[4096,256]{1,0:T(8,128)(2,1)}, ...), branch_computations={%region_13.14_spmd, %region_14.18_spmd} | conditional | flops 835764928 | bytes 26319488 | solution.py:104
  631.4 9.9 %all_gather.36 = bf16[64,4096]{1,0:T(8,128)(2,1)S(1)} all-gather(bf16[64,1024]{1,0:T(8,128)(2,1)S(1)} %bitcast_select_fusion.3), channel_id=1, replica_groups=mesh['dp'=32,'pipe'=2,'tensor'=4] {'tensor'}, dimensions={1}, use_global_device_ids=true | all-gather | bytes 655360 | tf_op jit(solution)/shard_map/while/body/eval_jaxpr/all_gather | solution.py:92
  648.8 11.3 %all-to-all-done = f32[4,64,1024]{2,1,0:T(8,128)S(1)} async-done(((f32[4,64,1024]{2,1,0:T(8,128)}), f32[4,64,1024]{2,1,0:T(8,128)S(1)}, u32[]{:S(2)}, u32[]{:S(2)}) %all-to-all-start) | async-done | bytes 1048608 | tf_op jit(solution)/shard_map/while/body/eval_jaxpr/all_to_all | solution.py:19
  661.0 10.7 %all_gather.37 = bf16[64,4096]{1,0:T(8,128)(2,1)S(1)} all-gather(bf16[64,1024]{1,0:T(8,128)(2,1)S(1)} %get-tuple-element.869), channel_id=1, replica_groups=mesh['dp'=32,'pipe'=2,'tensor'=4] {'tensor'}, dimensions={1}, use_global_device_ids=true | all-gather | bytes 655360 | tf_op jit(solution)/shard_map/while/body/eval_jaxpr/all_gather | solution.py:92
  687.5 26.7 %collective-permute-start.1 = (bf16[64,1024]{1,0:T(8,128)(2,1)S(1)}, bf16[64,1024]{1,0:T(8,128)(2,1)S(1)}, u32[]{:S(2)}, u32[]{:S(2)}) collective-permute-start(bf16[64,1024]{1,0:T(8,128)(2,1)S(1)} %get-tuple-element.870), channel_id=1, source_target_pairs={{4,0},{5,1},{6,2},{7,3},{12,8},{13,9},{14,10},{15,11},{20,16},{21,... | collective-permute-start | bytes 393224 | tf_op jit(solution)/shard_map/while/body/eval_jaxpr/ppermute | solution.py:33
  (248 shorter events, 204.7 us)
Async XLA Ops:
  6.5 11.5 %copy-start = (bf16[2,64,1024]{2,1,0:T(8,128)(2,1)S(1)}, bf16[2,64,1024]{2,1,0:T(8,128)(2,1)}, u32[]{:S(2)}) copy-start(bf16[2,64,1024]{2,1,0:T(8,128)(2,1)} %param.22) | copy-start | bytes 786436
  6.5 152.7 %all-gather.6.cloned.1.call-start = ((), (), s32[]{:S(2)}) async-start(), calls=%async_computation.3 | async-start | bytes 17301504 | tf_op jit(solution)/shard_map/all_gather | solution.py:146
  7.3 337.8 %all-gather.4.cloned.1.call-start = ((), (), s32[]{:S(2)}) async-start(), calls=%async_computation.2 | async-start | bytes 25952256 | tf_op jit(solution)/shard_map/all_gather | solution.py:26
  380.1 13.2 %all-to-all-start = ((f32[4,64,1024]{2,1,0:T(8,128)}), f32[4,64,1024]{2,1,0:T(8,128)S(1)}, u32[]{:S(2)}, u32[]{:S(2)}) async-start(f32[4,64,1024]{2,1,0:T(8,128)} %copy.113), calls=%async_computation | async-start | bytes 2097152 | tf_op jit(solution)/shard_map/while/body/eval_jaxpr/all_to_all | solution.py:19
  404.1 8.2 %copy-start.3 = (bf16[64,1024]{1,0:T(8,128)(2,1)S(1)}, bf16[64,1024]{1,0:T(8,128)(2,1)}, u32[]{:S(2)}) copy-start(bf16[64,1024]{1,0:T(8,128)(2,1)} %get-tuple-element.868) | copy-start | bytes 393220 | tf_op jit(solution)/shard_map/while
  406.5 13.5 %all-to-all-start.1 = ((f32[4,64,1024]{2,1,0:T(8,128)}), f32[4,64,1024]{2,1,0:T(8,128)S(1)}, u32[]{:S(2)}, u32[]{:S(2)}) async-start(f32[4,64,1024]{2,1,0:T(8,128)} %copy.114), calls=%async_computation.1 | async-start | bytes 2097152 | tf_op jit(solution)/shard_map/while/body/eval_jaxpr/all_to_all | solution.py:19
  412.3 34.6 %collective-permute-start = (bf16[64,1024]{1,0:T(8,128)(2,1)S(1)}, bf16[64,1024]{1,0:T(8,128)(2,1)}, u32[]{:S(2)}, u32[]{:S(2)}) collective-permute-start(bf16[64,1024]{1,0:T(8,128)(2,1)S(1)} %copy-done.3), channel_id=1, source_target_pairs={{0,4},{1,5},{2,6},{3,7},{8,12},{9,13},{10,14},{11,15},{16,20},{17,... | collective-permute-start | bytes 393224 | tf_op jit(solution)/shard_map/while/body/eval_jaxpr/ppermute | solution.py:33
  420.2 27.7 %collective-permute-start.1 = (bf16[64,1024]{1,0:T(8,128)(2,1)S(1)}, bf16[64,1024]{1,0:T(8,128)(2,1)S(1)}, u32[]{:S(2)}, u32[]{:S(2)}) collective-permute-start(bf16[64,1024]{1,0:T(8,128)(2,1)S(1)} %get-tuple-element.870), channel_id=1, source_target_pairs={{4,0},{5,1},{6,2},{7,3},{12,8},{13,9},{14,10},{15,11},{20,16},{21,... | collective-permute-start | bytes 393224 | tf_op jit(solution)/shard_map/while/body/eval_jaxpr/ppermute | solution.py:33
  479.0 14.9 %all-to-all-start = ((f32[4,64,1024]{2,1,0:T(8,128)}), f32[4,64,1024]{2,1,0:T(8,128)S(1)}, u32[]{:S(2)}, u32[]{:S(2)}) async-start(f32[4,64,1024]{2,1,0:T(8,128)} %copy.113), calls=%async_computation | async-start | bytes 2097152 | tf_op jit(solution)/shard_map/while/body/eval_jaxpr/all_to_all | solution.py:19
  516.9 10.9 %copy-start.8 = (s32[2]{0:T(128)S(1)}, s32[2]{0:T(128)}, u32[]{:S(2)}) copy-start(s32[2]{0:T(128)} %get-tuple-element.947) | copy-start | bytes 28 | tf_op jit(solution)/shard_map/while
  516.9 13.2 %copy-start.3 = (bf16[64,1024]{1,0:T(8,128)(2,1)S(1)}, bf16[64,1024]{1,0:T(8,128)(2,1)}, u32[]{:S(2)}) copy-start(bf16[64,1024]{1,0:T(8,128)(2,1)} %get-tuple-element.868) | copy-start | bytes 393220 | tf_op jit(solution)/shard_map/while
  524.3 13.2 %all-to-all-start.1 = ((f32[4,64,1024]{2,1,0:T(8,128)}), f32[4,64,1024]{2,1,0:T(8,128)S(1)}, u32[]{:S(2)}, u32[]{:S(2)}) async-start(f32[4,64,1024]{2,1,0:T(8,128)} %copy.114), calls=%async_computation.1 | async-start | bytes 2097152 | tf_op jit(solution)/shard_map/while/body/eval_jaxpr/all_to_all | solution.py:19
  530.1 8.9 %collective-permute-start = (bf16[64,1024]{1,0:T(8,128)(2,1)S(1)}, bf16[64,1024]{1,0:T(8,128)(2,1)}, u32[]{:S(2)}, u32[]{:S(2)}) collective-permute-start(bf16[64,1024]{1,0:T(8,128)(2,1)S(1)} %copy-done.3), channel_id=1, source_target_pairs={{0,4},{1,5},{2,6},{3,7},{8,12},{9,13},{10,14},{11,15},{16,20},{17,... | collective-permute-start | bytes 393224 | tf_op jit(solution)/shard_map/while/body/eval_jaxpr/ppermute | solution.py:33
  537.6 2.3 collective-permute-start.1
  571.0 14.2 %all-to-all-start = ((f32[4,64,1024]{2,1,0:T(8,128)}), f32[4,64,1024]{2,1,0:T(8,128)S(1)}, u32[]{:S(2)}, u32[]{:S(2)}) async-start(f32[4,64,1024]{2,1,0:T(8,128)} %copy.113), calls=%async_computation | async-start | bytes 2097152 | tf_op jit(solution)/shard_map/while/body/eval_jaxpr/all_to_all | solution.py:19
  607.4 10.9 %copy-start.8 = (s32[2]{0:T(128)S(1)}, s32[2]{0:T(128)}, u32[]{:S(2)}) copy-start(s32[2]{0:T(128)} %get-tuple-element.947) | copy-start | bytes 28 | tf_op jit(solution)/shard_map/while
  607.4 13.2 %copy-start.3 = (bf16[64,1024]{1,0:T(8,128)(2,1)S(1)}, bf16[64,1024]{1,0:T(8,128)(2,1)}, u32[]{:S(2)}) copy-start(bf16[64,1024]{1,0:T(8,128)(2,1)} %get-tuple-element.868) | copy-start | bytes 393220 | tf_op jit(solution)/shard_map/while
  614.7 13.2 %all-to-all-start.1 = ((f32[4,64,1024]{2,1,0:T(8,128)}), f32[4,64,1024]{2,1,0:T(8,128)S(1)}, u32[]{:S(2)}, u32[]{:S(2)}) async-start(f32[4,64,1024]{2,1,0:T(8,128)} %copy.114), calls=%async_computation.1 | async-start | bytes 2097152 | tf_op jit(solution)/shard_map/while/body/eval_jaxpr/all_to_all | solution.py:19
  620.5 8.9 %collective-permute-start = (bf16[64,1024]{1,0:T(8,128)(2,1)S(1)}, bf16[64,1024]{1,0:T(8,128)(2,1)}, u32[]{:S(2)}, u32[]{:S(2)}) collective-permute-start(bf16[64,1024]{1,0:T(8,128)(2,1)S(1)} %copy-done.3), channel_id=1, source_target_pairs={{0,4},{1,5},{2,6},{3,7},{8,12},{9,13},{10,14},{11,15},{16,20},{17,... | collective-permute-start | bytes 393224 | tf_op jit(solution)/shard_map/while/body/eval_jaxpr/ppermute | solution.py:33
  628.1 2.3 collective-permute-start.1
  645.3 14.9 %all-to-all-start = ((f32[4,64,1024]{2,1,0:T(8,128)}), f32[4,64,1024]{2,1,0:T(8,128)S(1)}, u32[]{:S(2)}, u32[]{:S(2)}) async-start(f32[4,64,1024]{2,1,0:T(8,128)} %copy.113), calls=%async_computation | async-start | bytes 2097152 | tf_op jit(solution)/shard_map/while/body/eval_jaxpr/all_to_all | solution.py:19
  674.1 13.2 %all-to-all-start.1 = ((f32[4,64,1024]{2,1,0:T(8,128)}), f32[4,64,1024]{2,1,0:T(8,128)S(1)}, u32[]{:S(2)}, u32[]{:S(2)}) async-start(f32[4,64,1024]{2,1,0:T(8,128)} %copy.114), calls=%async_computation.1 | async-start | bytes 2097152 | tf_op jit(solution)/shard_map/while/body/eval_jaxpr/all_to_all | solution.py:19
  679.9 34.3 %collective-permute-start = (bf16[64,1024]{1,0:T(8,128)(2,1)S(1)}, bf16[64,1024]{1,0:T(8,128)(2,1)}, u32[]{:S(2)}, u32[]{:S(2)}) collective-permute-start(bf16[64,1024]{1,0:T(8,128)(2,1)S(1)} %copy-done.3), channel_id=1, source_target_pairs={{0,4},{1,5},{2,6},{3,7},{8,12},{9,13},{10,14},{11,15},{16,20},{17,... | collective-permute-start | bytes 393224 | tf_op jit(solution)/shard_map/while/body/eval_jaxpr/ppermute | solution.py:33
  687.5 27.7 %collective-permute-start.1 = (bf16[64,1024]{1,0:T(8,128)(2,1)S(1)}, bf16[64,1024]{1,0:T(8,128)(2,1)S(1)}, u32[]{:S(2)}, u32[]{:S(2)}) collective-permute-start(bf16[64,1024]{1,0:T(8,128)(2,1)S(1)} %get-tuple-element.870), channel_id=1, source_target_pairs={{4,0},{5,1},{6,2},{7,3},{12,8},{13,9},{14,10},{15,11},{20,16},{21,... | collective-permute-start | bytes 393224 | tf_op jit(solution)/shard_map/while/body/eval_jaxpr/ppermute | solution.py:33
  (13 other events, 56.3 us)
Sparse Core Ops, SparseCore 0:
  9.8 149.3 all-gather.5
  161.8 183.1 all-gather.3
where the time goes:
time: 727 us; the launch traced here: 725 us
  waiting for transfers between devices  383 us (53%)
  starting transfers between devices  89.4 us (12%)
  blocking collectives  84.6 us (12%)
  local copies, waits for them, and re-layouts  62.1 us (9%)
  matrix products  60.5 us (8%)
  other arithmetic  24 us (3%)
  between operations  13.5 us (2%)
  loops' own time  8.27 us (1%)
    all_gather x1, waiting for transfers between devices, sent_together(): whole = lax.all_gather(both, axis, axis=dim, tiled=True)  174 us
    all_gather x1, waiting for transfers between devices, per_device(): out_full = lax.all_gather(w_out, 'dp', axis=3, tiled=True)  136 us
    all_gather x8, blocking collectives, layer_step(): gathered = lax.all_gather(stream, 'tensor', axis=1, tiled=True)  82.3 us
    all_to_all x8, waiting for transfers between devices, sent_and_summed(): lax.all_to_all(cut_along(value, dim, peers), axis, 0, 0, tiled=True)  67.7 us
    ppermute x8, starting transfers between devices, from_behind(): return lax.ppermute(value, axis, pairs)  61.2 us
    all_to_all x8, starting transfers between devices, sent_and_summed(): lax.all_to_all(cut_along(value, dim, peers), axis, 0, 0, tiled=True)  28.1 us
    dot_general x4, matrix products, attend(): queries = jnp.dot(normed, q_weight, preferred_element_type=jnp.float32)  20.3 us
    dot_general x4, matrix products, layer_step(): jnp.dot(mixed, out_part, preferred_element_type=jnp.float32)  19.8 us
  transfers between devices with their start and end apart: 18, of which 14 were waited for; matrix products, arithmetic and copies ran while one was open for 4% of the time, Pallas kernels for 0%

commit v1 on v0

--- a/solution.py
+++ b/solution.py
@@ -143,7 +143,8 @@
     angles = rope_angles(positions, HEAD_DIM)
     down_gain = norm_gain[0, 0]
     up_gain = norm_gain[1, 0]
-    out_full = lax.all_gather(w_out, "dp", axis=3, tiled=True)
+    sent = jnp.stack([w_out] * lax.axis_size("dp"))
+    out_full = jnp.concatenate(lax.all_to_all(sent, "dp", 0, 0), axis=3)
     down_out_part = out_full[0, 0]
     up_out_part = out_full[1, 0]
     query_full, key_full, value_full = sent_together((w_query, w_key, w_value), "dp", 2, 3)

time: 727 us -> 991 us (1.36)
  the two profiles are of different devices: /device:TPU:1 before, /device:TPU:199 now
where the time goes in v1:
time: 991 us; the launch traced here: 988 us
  waiting for transfers between devices  591 us (60%)
  local copies, waits for them, and re-layouts  111 us (11%)
  starting transfers between devices  98.3 us (10%)
  blocking collectives  83 us (8%)
  matrix products  60.4 us (6%)
  other arithmetic  22.1 us (2%)
  between operations  13.5 us (1%)
    all_to_all x1, waiting for transfers between devices, per_device(): out_full = jnp.concatenate(lax.all_to_all(sent, 'dp', 0, 0), axis=3)  520 us
    all_gather x8, blocking collectives, layer_step(): gathered = lax.all_gather(stream, 'tensor', axis=1, tiled=True)  80.7 us
    all_to_all x8, waiting for transfers between devices, sent_and_summed(): lax.all_to_all(cut_along(value, dim, peers), axis, 0, 0, tiled=True)  66.5 us
    ppermute x8, starting transfers between devices, from_behind(): return lax.ppermute(value, axis, pairs)  61.7 us
    all_to_all x8, starting transfers between devices, sent_and_summed(): lax.all_to_all(cut_along(value, dim, peers), axis, 0, 0, tiled=True)  28.1 us
    unnamed x18, local copies, waits for them, and re-layouts  23.5 us
    all_to_all x1, local copies, waits for them, and re-layouts, per_device(): out_full = jnp.concatenate(lax.all_to_all(sent, 'dp', 0, 0), axis=3)  21.2 us
    dot_general x4, matrix products, attend(): queries = jnp.dot(normed, q_weight, preferred_element_type=jnp.float32)  20.3 us
  transfers between devices with their start and end apart: 18, of which 13 were waited for; matrix products, arithmetic and copies ran while one was open for 8% of the time, Pallas kernels for 0%

profile of v1, /device:TPU:199, one launch (start us, length us, event | category | flops | bytes accessed | tf_op | source)
XLA Modules:
  0.0 988.0 jit_solution(6784506779217757122)
XLA Ops:
  32.4 520.5 %all-to-all-done.2 = bf16[32,2,1,1024,128]{4,3,2,1,0:T(8,128)(2,1)} async-done(((bf16[32,2,1,1024,128]{4,3,2,1,0:T(8,128)(2,1)}), bf16[32,2,1,1024,128]{4,3,2,1,0:T(8,128)(2,1)}, u32[]{:S(2)}, u32[]{:S(2)}) %all-to-all-start.2) | async-done | bytes 16777248 | tf_op jit(solution)/shard_map/all_to_all | solution.py:147
  552.8 21.2 %copy.86 = bf16[32,2,1,1024,128]{3,4,0,2,1:T(8,128)(2,1)} copy(bf16[32,2,1,1024,128]{4,3,2,1,0:T(8,128)(2,1)} %all-to-all-done.2) | data formatting | bytes 33554432 | tf_op jit(solution)/shard_map/all_to_all | solution.py:147
  574.0 11.9 %fusion.99 = (bf16[1,1,1024,32,128]{2,4,3,1,0:T(8,128)(2,1)}, bf16[1,1,1024,32,128]{2,4,3,1,0:T(8,128)(2,1)}) fusion(bf16[2,1,1024,32,128]{2,4,3,1,0:T(8,128)(2,1)} %bitcast.140), kind=kLoop, calls=%fused_computation.131 | loop fusion | bytes 33554432 | tf_op jit(solution)/shard_map/slice | solution.py:149
  585.9 12.0 %copy.87 = bf16[1024,4096]{1,0:T(8,128)(2,1)} copy(bf16[1024,4096]{0,1:T(8,128)(2,1)} %bitcast.144) | data formatting | bytes 16777216
  597.9 11.4 %copy.88 = bf16[1024,4096]{1,0:T(8,128)(2,1)} copy(bf16[1024,4096]{0,1:T(8,128)(2,1)} %bitcast.143) | data formatting | bytes 16777216
  615.7 11.6 %slice_bitcast_fusion = (bf16[4096,1024]{1,0:T(8,128)(2,1)}, bf16[4096,1024]{1,0:T(8,128)(2,1)}) fusion(bf16[2,1,4096,1536]{3,2,1,0:T(8,128)(2,1)} %all-gather.3.cloned.1.call-done), kind=kLoop, calls=%fused_computation.98 | loop fusion | bytes 33554432 | tf_op jit(solution)/shard_map/squeeze | solution.py:152
  628.0 350.2 %while.19 = (s32[]{:T(128)}, bf16[64,1024]{1,0:T(8,128)(2,1)}, bf16[64,1024]{1,0:T(8,128)(2,1)S(1)}, bf16[2,64,1024]{2,1,0:T(8,128)(2,1)S(1)}, s32[]{:T(128)}, /...) while((s32[]{:T(128)}, bf16[64,1024]{1,0:T(8,128)(2,1)}, ...), condition=%wide.region_21.23_spmd.clone, body=%wide.region_4.22_spmd.clone.sunk | while | flops 2746410496 | bytes 85502200 | solution.py:201
  629.2 9.9 %all_gather.32 = bf16[64,4096]{1,0:T(8,128)(2,1)S(1)} all-gather(bf16[64,1024]{1,0:T(8,128)(2,1)S(1)} %bitcast_select_fusion.3), channel_id=1, replica_groups=mesh['dp'=32,'pipe'=2,'tensor'=4] {'tensor'}, dimensions={1}, use_global_device_ids=true | all-gather | bytes 655360 | tf_op jit(solution)/shard_map/while/body/eval_jaxpr/all_gather | solution.py:92
  657.2 9.9 %all_gather.33 = bf16[64,4096]{1,0:T(8,128)(2,1)S(1)} all-gather(bf16[64,1024]{1,0:T(8,128)(2,1)S(1)} %get-tuple-element.917), channel_id=1, replica_groups=mesh['dp'=32,'pipe'=2,'tensor'=4] {'tensor'}, dimensions={1}, use_global_device_ids=true | all-gather | bytes 655360 | tf_op jit(solution)/shard_map/while/body/eval_jaxpr/all_gather | solution.py:92
  682.9 27.2 %collective-permute-start.1 = (bf16[64,1024]{1,0:T(8,128)(2,1)S(1)}, bf16[64,1024]{1,0:T(8,128)(2,1)S(1)}, u32[]{:S(2)}, u32[]{:S(2)}) collective-permute-start(bf16[64,1024]{1,0:T(8,128)(2,1)S(1)} %get-tuple-element.918), channel_id=1, source_target_pairs={{4,0},{5,1},{6,2},{7,3},{12,8},{13,9},{14,10},{15,11},{20,16},{21,... | collective-permute-start | bytes 393224 | tf_op jit(solution)/shard_map/while/body/eval_jaxpr/ppermute | solution.py:33
  712.1 9.9 %all_gather.32 = bf16[64,4096]{1,0:T(8,128)(2,1)S(1)} all-gather(bf16[64,1024]{1,0:T(8,128)(2,1)S(1)} %bitcast_select_fusion.3), channel_id=1, replica_groups=mesh['dp'=32,'pipe'=2,'tensor'=4] {'tensor'}, dimensions={1}, use_global_device_ids=true | all-gather | bytes 655360 | tf_op jit(solution)/shard_map/while/body/eval_jaxpr/all_gather | solution.py:92
  723.7 11.3 %conditional.12 = (bf16[64,1024]{1,0:T(8,128)(2,1)S(1)}) conditional(s32[]{:T(128)} %convert_element_type.206, () %tuple.109, (bf16[64,4096]{1,0:T(8,128)(2,1)S(1)}, f32[1,1,4096]{2,1,0:T(1,128)S(1)}, bf16[4096,256]{1,0:T(8,128)(2,1)}, s32[]{:T(128)}, pred[2,64,64]{1,2,0:T(8,128)(4,1)S(1)}, /*index=5*/bf16[4096,256]{1,0:T(8,128)(2,1)}, ...), branch_computations={%region_5.6_spmd, %region_6.10_spmd} | conditional | flops 835764928 | bytes 17847848 | solution.py:104
  745.8 11.3 %all-to-all-done = f32[4,64,1024]{2,1,0:T(8,128)S(1)} async-done(((f32[4,64,1024]{2,1,0:T(8,128)}), f32[4,64,1024]{2,1,0:T(8,128)S(1)}, u32[]{:S(2)}, u32[]{:S(2)}) %all-to-all-start) | async-done | bytes 1048608 | tf_op jit(solution)/shard_map/while/body/eval_jaxpr/all_to_all | solution.py:19
  757.9 10.7 %all_gather.33 = bf16[64,4096]{1,0:T(8,128)(2,1)S(1)} all-gather(bf16[64,1024]{1,0:T(8,128)(2,1)S(1)} %get-tuple-element.917), channel_id=1, replica_groups=mesh['dp'=32,'pipe'=2,'tensor'=4] {'tensor'}, dimensions={1}, use_global_device_ids=true | all-gather | bytes 655360 | tf_op jit(solution)/shard_map/while/body/eval_jaxpr/all_gather | solution.py:92
  768.6 11.5 %conditional.14 = (bf16[64,1024]{1,0:T(8,128)(2,1)S(1)}) conditional(s32[]{:T(128)} %convert_element_type.207, () %tuple.113, (bf16[64,4096]{1,0:T(8,128)(2,1)S(1)}, f32[1,1,4096]{2,1,0:T(1,128)S(1)}, bf16[4096,256]{1,0:T(8,128)(2,1)}, pred[2,64,64]{1,2,0:T(8,128)(4,1)S(1)}, s32[]{:T(128)}, /*index=5*/bf16[4096,256]{1,0:T(8,128)(2,1)}, ...), branch_computations={%region_13.14_spmd, %region_14.18_spmd} | conditional | flops 835764928 | bytes 26319488 | solution.py:104
  804.0 9.9 %all_gather.32 = bf16[64,4096]{1,0:T(8,128)(2,1)S(1)} all-gather(bf16[64,1024]{1,0:T(8,128)(2,1)S(1)} %bitcast_select_fusion.3), channel_id=1, replica_groups=mesh['dp'=32,'pipe'=2,'tensor'=4] {'tensor'}, dimensions={1}, use_global_device_ids=true | all-gather | bytes 655360 | tf_op jit(solution)/shard_map/while/body/eval_jaxpr/all_gather | solution.py:92
  815.6 11.3 %conditional.12 = (bf16[64,1024]{1,0:T(8,128)(2,1)S(1)}) conditional(s32[]{:T(128)} %convert_element_type.206, () %tuple.109, (bf16[64,4096]{1,0:T(8,128)(2,1)S(1)}, f32[1,1,4096]{2,1,0:T(1,128)S(1)}, bf16[4096,256]{1,0:T(8,128)(2,1)}, s32[]{:T(128)}, pred[2,64,64]{1,2,0:T(8,128)(4,1)S(1)}, /*index=5*/bf16[4096,256]{1,0:T(8,128)(2,1)}, ...), branch_computations={%region_5.6_spmd, %region_6.10_spmd} | conditional | flops 835764928 | bytes 17847848 | solution.py:104
  837.7 10.6 %all-to-all-done = f32[4,64,1024]{2,1,0:T(8,128)S(1)} async-done(((f32[4,64,1024]{2,1,0:T(8,128)}), f32[4,64,1024]{2,1,0:T(8,128)S(1)}, u32[]{:S(2)}, u32[]{:S(2)}) %all-to-all-start) | async-done | bytes 1048608 | tf_op jit(solution)/shard_map/while/body/eval_jaxpr/all_to_all | solution.py:19
  849.1 9.9 %all_gather.33 = bf16[64,4096]{1,0:T(8,128)(2,1)S(1)} all-gather(bf16[64,1024]{1,0:T(8,128)(2,1)S(1)} %get-tuple-element.917), channel_id=1, replica_groups=mesh['dp'=32,'pipe'=2,'tensor'=4] {'tensor'}, dimensions={1}, use_global_device_ids=true | all-gather | bytes 655360 | tf_op jit(solution)/shard_map/while/body/eval_jaxpr/all_gather | solution.py:92
  859.0 11.5 %conditional.14 = (bf16[64,1024]{1,0:T(8,128)(2,1)S(1)}) conditional(s32[]{:T(128)} %convert_element_type.207, () %tuple.113, (bf16[64,4096]{1,0:T(8,128)(2,1)S(1)}, f32[1,1,4096]{2,1,0:T(1,128)S(1)}, bf16[4096,256]{1,0:T(8,128)(2,1)}, pred[2,64,64]{1,2,0:T(8,128)(4,1)S(1)}, s32[]{:T(128)}, /*index=5*/bf16[4096,256]{1,0:T(8,128)(2,1)}, ...), branch_computations={%region_13.14_spmd, %region_14.18_spmd} | conditional | flops 835764928 | bytes 26319488 | solution.py:104
  894.4 9.9 %all_gather.32 = bf16[64,4096]{1,0:T(8,128)(2,1)S(1)} all-gather(bf16[64,1024]{1,0:T(8,128)(2,1)S(1)} %bitcast_select_fusion.3), channel_id=1, replica_groups=mesh['dp'=32,'pipe'=2,'tensor'=4] {'tensor'}, dimensions={1}, use_global_device_ids=true | all-gather | bytes 655360 | tf_op jit(solution)/shard_map/while/body/eval_jaxpr/all_gather | solution.py:92
  911.9 11.3 %all-to-all-done = f32[4,64,1024]{2,1,0:T(8,128)S(1)} async-done(((f32[4,64,1024]{2,1,0:T(8,128)}), f32[4,64,1024]{2,1,0:T(8,128)S(1)}, u32[]{:S(2)}, u32[]{:S(2)}) %all-to-all-start) | async-done | bytes 1048608 | tf_op jit(solution)/shard_map/while/body/eval_jaxpr/all_to_all | solution.py:19
  924.0 10.7 %all_gather.33 = bf16[64,4096]{1,0:T(8,128)(2,1)S(1)} all-gather(bf16[64,1024]{1,0:T(8,128)(2,1)S(1)} %get-tuple-element.917), channel_id=1, replica_groups=mesh['dp'=32,'pipe'=2,'tensor'=4] {'tensor'}, dimensions={1}, use_global_device_ids=true | all-gather | bytes 655360 | tf_op jit(solution)/shard_map/while/body/eval_jaxpr/all_gather | solution.py:92
  950.5 26.7 %collective-permute-start.1 = (bf16[64,1024]{1,0:T(8,128)(2,1)S(1)}, bf16[64,1024]{1,0:T(8,128)(2,1)S(1)}, u32[]{:S(2)}, u32[]{:S(2)}) collective-permute-start(bf16[64,1024]{1,0:T(8,128)(2,1)S(1)} %get-tuple-element.918), channel_id=1, source_target_pairs={{4,0},{5,1},{6,2},{7,3},{12,8},{13,9},{14,10},{15,11},{20,16},{21,... | collective-permute-start | bytes 393224 | tf_op jit(solution)/shard_map/while/body/eval_jaxpr/ppermute | solution.py:33
  (261 shorter events, 229.0 us)
Async XLA Ops:
  6.5 21.7 %copy-start = (bf16[2,64,1024]{2,1,0:T(8,128)(2,1)S(1)}, bf16[2,64,1024]{2,1,0:T(8,128)(2,1)}, u32[]{:S(2)}) copy-start(bf16[2,64,1024]{2,1,0:T(8,128)(2,1)} %param.22) | copy-start | bytes 786436
  6.5 602.8 %all-gather.3.cloned.1.call-start = ((), (), s32[]{:S(2)}) async-start(), calls=%async_computation.3 | async-start | bytes 25952256 | tf_op jit(solution)/shard_map/all_gather | solution.py:26
  15.7 11.2 %copy-start.3 = (s32[2]{0:T(128)S(1)}, s32[2]{0:T(128)}, u32[]{:S(2)}) copy-start(s32[2]{0:T(128)} %param.28) | copy-start | bytes 28
  15.7 11.9 %copy-start.4 = (s32[2]{0:T(128)S(1)}, s32[2]{0:T(128)}, u32[]{:S(2)}) copy-start(s32[2]{0:T(128)} %param.29) | copy-start | bytes 28
  15.7 16.6 %copy-start.11 = (f32[2,1,4096]{2,1,0:T(1,128)S(1)}, f32[2,1,4096]{2,1,0:T(1,128)}, u32[]{:S(2)}) copy-start(f32[2,1,4096]{2,1,0:T(1,128)} %param.27) | copy-start | bytes 98308
  15.7 537.1 %all-to-all-start.2 = ((bf16[32,2,1,1024,128]{4,3,2,1,0:T(8,128)(2,1)}), bf16[32,2,1,1024,128]{4,3,2,1,0:T(8,128)(2,1)}, u32[]{:S(2)}, u32[]{:S(2)}) async-start(bf16[32,2,1,1024,128]{4,3,2,1,0:T(8,128)(2,1)} %stack.2), calls=%async_computation.2 | async-start | bytes 33554432 | tf_op jit(solution)/shard_map/all_to_all | solution.py:147
  643.2 13.2 %all-to-all-start = ((f32[4,64,1024]{2,1,0:T(8,128)}), f32[4,64,1024]{2,1,0:T(8,128)S(1)}, u32[]{:S(2)}, u32[]{:S(2)}) async-start(f32[4,64,1024]{2,1,0:T(8,128)} %copy.119), calls=%async_computation | async-start | bytes 2097152 | tf_op jit(solution)/shard_map/while/body/eval_jaxpr/all_to_all | solution.py:19
  669.5 13.3 %all-to-all-start.1 = ((f32[4,64,1024]{2,1,0:T(8,128)}), f32[4,64,1024]{2,1,0:T(8,128)S(1)}, u32[]{:S(2)}, u32[]{:S(2)}) async-start(f32[4,64,1024]{2,1,0:T(8,128)} %copy.120), calls=%async_computation.1 | async-start | bytes 2097152 | tf_op jit(solution)/shard_map/while/body/eval_jaxpr/all_to_all | solution.py:19
  675.6 34.6 %collective-permute-start = (bf16[64,1024]{1,0:T(8,128)(2,1)S(1)}, bf16[64,1024]{1,0:T(8,128)(2,1)}, u32[]{:S(2)}, u32[]{:S(2)}) collective-permute-start(bf16[64,1024]{1,0:T(8,128)(2,1)S(1)} %copy-done.6), channel_id=1, source_target_pairs={{0,4},{1,5},{2,6},{3,7},{8,12},{9,13},{10,14},{11,15},{16,20},{17,... | collective-permute-start | bytes 393224 | tf_op jit(solution)/shard_map/while/body/eval_jaxpr/ppermute | solution.py:33
  682.9 28.2 %collective-permute-start.1 = (bf16[64,1024]{1,0:T(8,128)(2,1)S(1)}, bf16[64,1024]{1,0:T(8,128)(2,1)S(1)}, u32[]{:S(2)}, u32[]{:S(2)}) collective-permute-start(bf16[64,1024]{1,0:T(8,128)(2,1)S(1)} %get-tuple-element.918), channel_id=1, source_target_pairs={{4,0},{5,1},{6,2},{7,3},{12,8},{13,9},{14,10},{15,11},{20,16},{21,... | collective-permute-start | bytes 393224 | tf_op jit(solution)/shard_map/while/body/eval_jaxpr/ppermute | solution.py:33
  742.2 14.9 %all-to-all-start = ((f32[4,64,1024]{2,1,0:T(8,128)}), f32[4,64,1024]{2,1,0:T(8,128)S(1)}, u32[]{:S(2)}, u32[]{:S(2)}) async-start(f32[4,64,1024]{2,1,0:T(8,128)} %copy.119), calls=%async_computation | async-start | bytes 2097152 | tf_op jit(solution)/shard_map/while/body/eval_jaxpr/all_to_all | solution.py:19
  780.1 13.4 %copy-start.6 = (bf16[64,1024]{1,0:T(8,128)(2,1)S(1)}, bf16[64,1024]{1,0:T(8,128)(2,1)}, u32[]{:S(2)}) copy-start(bf16[64,1024]{1,0:T(8,128)(2,1)} %get-tuple-element.916) | copy-start | bytes 393220 | tf_op jit(solution)/shard_map/while
  787.4 13.2 %all-to-all-start.1 = ((f32[4,64,1024]{2,1,0:T(8,128)}), f32[4,64,1024]{2,1,0:T(8,128)S(1)}, u32[]{:S(2)}, u32[]{:S(2)}) async-start(f32[4,64,1024]{2,1,0:T(8,128)} %copy.120), calls=%async_computation.1 | async-start | bytes 2097152 | tf_op jit(solution)/shard_map/while/body/eval_jaxpr/all_to_all | solution.py:19
  793.5 8.6 collective-permute-start
  800.8 2.3 collective-permute-start.1
  834.1 14.2 %all-to-all-start = ((f32[4,64,1024]{2,1,0:T(8,128)}), f32[4,64,1024]{2,1,0:T(8,128)S(1)}, u32[]{:S(2)}, u32[]{:S(2)}) async-start(f32[4,64,1024]{2,1,0:T(8,128)} %copy.119), calls=%async_computation | async-start | bytes 2097152 | tf_op jit(solution)/shard_map/while/body/eval_jaxpr/all_to_all | solution.py:19
  870.5 13.4 %copy-start.6 = (bf16[64,1024]{1,0:T(8,128)(2,1)S(1)}, bf16[64,1024]{1,0:T(8,128)(2,1)}, u32[]{:S(2)}) copy-start(bf16[64,1024]{1,0:T(8,128)(2,1)} %get-tuple-element.916) | copy-start | bytes 393220 | tf_op jit(solution)/shard_map/while
  877.8 13.2 %all-to-all-start.1 = ((f32[4,64,1024]{2,1,0:T(8,128)}), f32[4,64,1024]{2,1,0:T(8,128)S(1)}, u32[]{:S(2)}, u32[]{:S(2)}) async-start(f32[4,64,1024]{2,1,0:T(8,128)} %copy.120), calls=%async_computation.1 | async-start | bytes 2097152 | tf_op jit(solution)/shard_map/while/body/eval_jaxpr/all_to_all | solution.py:19
  883.8 8.6 collective-permute-start
  891.1 2.3 collective-permute-start.1
  908.4 14.9 %all-to-all-start = ((f32[4,64,1024]{2,1,0:T(8,128)}), f32[4,64,1024]{2,1,0:T(8,128)S(1)}, u32[]{:S(2)}, u32[]{:S(2)}) async-start(f32[4,64,1024]{2,1,0:T(8,128)} %copy.119), calls=%async_computation | async-start | bytes 2097152 | tf_op jit(solution)/shard_map/while/body/eval_jaxpr/all_to_all | solution.py:19
  937.2 13.2 %all-to-all-start.1 = ((f32[4,64,1024]{2,1,0:T(8,128)}), f32[4,64,1024]{2,1,0:T(8,128)S(1)}, u32[]{:S(2)}, u32[]{:S(2)}) async-start(f32[4,64,1024]{2,1,0:T(8,128)} %copy.120), calls=%async_computation.1 | async-start | bytes 2097152 | tf_op jit(solution)/shard_map/while/body/eval_jaxpr/all_to_all | solution.py:19
  943.2 34.0 %collective-permute-start = (bf16[64,1024]{1,0:T(8,128)(2,1)S(1)}, bf16[64,1024]{1,0:T(8,128)(2,1)}, u32[]{:S(2)}, u32[]{:S(2)}) collective-permute-start(bf16[64,1024]{1,0:T(8,128)(2,1)S(1)} %copy-done.6), channel_id=1, source_target_pairs={{0,4},{1,5},{2,6},{3,7},{8,12},{9,13},{10,14},{11,15},{16,20},{17,... | collective-permute-start | bytes 393224 | tf_op jit(solution)/shard_map/while/body/eval_jaxpr/ppermute | solution.py:33
  950.5 27.6 %collective-permute-start.1 = (bf16[64,1024]{1,0:T(8,128)(2,1)S(1)}, bf16[64,1024]{1,0:T(8,128)(2,1)S(1)}, u32[]{:S(2)}, u32[]{:S(2)}) collective-permute-start(bf16[64,1024]{1,0:T(8,128)(2,1)S(1)} %get-tuple-element.918), channel_id=1, source_target_pairs={{4,0},{5,1},{6,2},{7,3},{12,8},{13,9},{14,10},{15,11},{20,16},{21,... | collective-permute-start | bytes 393224 | tf_op jit(solution)/shard_map/while/body/eval_jaxpr/ppermute | solution.py:33
  (18 other events, 102.0 us)
Sparse Core Ops, SparseCore 0:
  9.9 538.8 all-gather.2
